TPU v7x, 512 devices: a whole 4x8x8 slice. The times are simulated.
512 devices in a mesh: mid: 128 (over x, y, z_hi, core), sub: 4 (over z_lo).
Axes of the slice: x: 4, y: 8, z: 8 (z_hi: 2, z_lo: 4; z = z_hi * 4 + z_lo), core: 2. Of those that a mesh axis runs over, the one named last changes fastest.
Arguments:
- signal: bfloat16 [393216, 1152], P(('mid', 'sub')), may hold values from -6 to 6
- col_basis: bfloat16 [393216, 256], P(('mid', 'sub')), may hold values from -0.21875 to 0.21875
- right_coupling: bfloat16 [512, 2, 256, 256], P(('mid', 'sub')), may hold values from -0.375 to 0.375
- middle_coupling: bfloat16 [512, 256, 256], P(('mid', 'sub')), may hold values from -0.375 to 0.375
- left_coupling: bfloat16 [512, 2, 256, 256], P(('mid', 'sub')), may hold values from -0.375 to 0.375
- row_basis: bfloat16 [393216, 256], P(('mid', 'sub')), may hold values from -0.375 to 0.375
- node_order: int32 [128], replicated, may hold values from 0 to 127, each once
Outputs:
- product: bfloat16 [393216, 1152], P(('mid', 'sub'))
Inputs may be any that keep to these rules, and one draw needn't show every extreme that they name: node_order holds each of 0 to 127 exactly once.
All inputs are finite; a program needn't handle non-finite values.
Results may differ from a plain program's by a relative error of at most 0.013.
Values may be sent and summed in bfloat16 or wider, within the bound.
A program may use at most 64 MiB of HBM per device.

v0:
```python
import jax
import jax.numpy as jnp
from jax import lax
from jax.sharding import PartitionSpec as P


def from_partner(block, axis, distance):
    count = lax.axis_size(axis)
    route = []
    for low in range(count):
        high = low | 1 << distance
        if high != low and high < count:
            route += [(low, high), (high, low)]
    return lax.ppermute(block, axis, route)


def stack_halves(coeffs, received, bitval):
    half = coeffs.shape[0] // 2
    keep = jnp.where(bitval == 1, coeffs[half:], coeffs[:half])
    return jnp.where(
        bitval == 1,
        jnp.concatenate([received, keep], axis=0),
        jnp.concatenate([keep, received], axis=0),
    )


def outgoing(coeffs, bitval):
    half = coeffs.shape[0] // 2
    return jnp.where(bitval == 1, coeffs[:half], coeffs[half:])


def chain(
    signal_blk, col_basis, right_coupling, middle_coupling, left_coupling, row_basis, node_order
):
    position = lax.axis_index("sub")
    width = col_basis.shape[1]
    groups = lax.axis_size("mid")
    coeffs = lax.dot_general(
        col_basis, signal_blk, (((0,), (0,)), ((), ())), preferred_element_type=jnp.float32
    ).astype(jnp.bfloat16)
    for level, bit in ((0, 0), (1, 1)):
        bitval = position >> bit & 1
        received = from_partner(outgoing(coeffs, bitval), "sub", bit)
        stacked = stack_halves(coeffs, received, bitval)
        coeffs = jnp.dot(
            right_coupling[0, level], stacked, preferred_element_type=jnp.float32
        ).astype(jnp.bfloat16)
    pieces = coeffs.reshape(groups, width // groups, coeffs.shape[1])
    ordered = jnp.take(pieces, node_order, axis=0)
    arrived = lax.all_to_all(ordered, "mid", split_axis=0, concat_axis=0, tiled=True)
    flat = arrived.reshape(width, arrived.shape[2])
    coeffs = jnp.dot(middle_coupling[0], flat, preferred_element_type=jnp.float32).astype(
        jnp.bfloat16
    )
    for level, bit in ((0, 1), (1, 0)):
        bitval = position >> bit & 1
        received = from_partner(outgoing(coeffs, bitval), "sub", bit)
        stacked = stack_halves(coeffs, received, bitval)
        coeffs = jnp.dot(
            left_coupling[0, level], stacked, preferred_element_type=jnp.float32
        ).astype(jnp.bfloat16)
    return jnp.dot(row_basis, coeffs, preferred_element_type=jnp.float32).astype(jnp.bfloat16)


def local(signal, col_basis, right_coupling, middle_coupling, left_coupling, row_basis, node_order):
    return chain(
        signal, col_basis, right_coupling, middle_coupling, left_coupling, row_basis, node_order
    )


def solution(mesh):
    return jax.shard_map(
        local,
        mesh=mesh,
        in_specs=(
            P(("mid", "sub"), None),
            P(("mid", "sub"), None),
            P(("mid", "sub"), None, None, None),
            P(("mid", "sub"), None, None),
            P(("mid", "sub"), None, None, None),
            P(("mid", "sub"), None),
            P(),
        ),
        out_specs=P(("mid", "sub"), None),
        check_vma=False,
    )
```

profile of v0, /device:TPU:1, one launch (start us, length us, event | category | flops | bytes accessed | tf_op | source)
XLA Modules:
  0.0 113.1 jit_solution(18082071240564462309)
XLA Ops:
  0.0 0.0 copy-start
  0.0 1.5 %copy-done = bf16[768,1152]{1,0:T(8,128)(2,1)S(1)} copy-done((bf16[768,1152]{1,0:T(8,128)(2,1)S(1)}, bf16[768,1152]{1,0:T(8,128)(2,1)}, u32[]{:S(2)}) %copy-start) | copy-done | bytes 1769496
  1.5 1.7 %convolution_convert_fusion.6 = bf16[256,1152]{1,0:T(8,128)(2,1)S(1)} fusion(bf16[768,256]{1,0:T(8,128)(2,1)} %param.8, bf16[768,1152]{1,0:T(8,128)(2,1)S(1)} %copy-done), kind=kOutput, calls=%fused_computation.8 | convolution fusion | flops 453279744 | bytes 2752512 | tf_op jit(solution)/shard_map/dot_general | solution.py:38
  3.2 0.0 copy-start.5
  3.2 0.0 copy-start.3
  3.2 0.1 broadcast_select_fusion.8
  3.3 4.8 %collective-permute-start = (bf16[128,1152]{1,0:T(8,128)(2,1)S(1)}, bf16[128,1152]{1,0:T(8,128)(2,1)S(1)}, u32[]{:S(2)}, u32[]{:S(2)}) collective-permute-start(bf16[128,1152]{1,0:T(8,128)(2,1)S(1)} %get-tuple-element.11), channel_id=1, source_target_pairs={{0,1},{1,0},{2,3},{3,2},{4,5},{5,4},{6,7},{7,6},{8,9},{9,8},{10,11... | collective-permute-start | bytes 884744 | tf_op jit(solution)/shard_map/ppermute | solution.py:14
  8.1 0.0 copy-done.5
  8.1 4.1 %collective-permute-done = bf16[128,1152]{1,0:T(8,128)(2,1)S(1)} collective-permute-done((bf16[128,1152]{1,0:T(8,128)(2,1)S(1)}, bf16[128,1152]{1,0:T(8,128)(2,1)S(1)}, u32[]{:S(2)}, u32[]{:S(2)}) %collective-permute-start) | collective-permute-done | bytes 294944 | tf_op jit(solution)/shard_map/ppermute | solution.py:14
  12.2 0.0 copy-done.3
  12.2 0.4 fusion.1
  12.6 0.1 broadcast_select_fusion.4
  12.6 8.4 %collective-permute-start.1 = (bf16[128,1152]{1,0:T(8,128)(2,1)S(1)}, bf16[128,1152]{1,0:T(8,128)(2,1)S(1)}, u32[]{:S(2)}, u32[]{:S(2)}) collective-permute-start(bf16[128,1152]{1,0:T(8,128)(2,1)S(1)} %get-tuple-element.9), channel_id=1, source_target_pairs={{0,2},{2,0},{1,3},{3,1},{4,6},{6,4},{5,7},{7,5},{8,10},{10,8},{9,1... | collective-permute-start | bytes 884744 | tf_op jit(solution)/shard_map/ppermute | solution.py:14
  21.1 12.9 %collective-permute-done.1 = bf16[128,1152]{1,0:T(8,128)(2,1)S(1)} collective-permute-done((bf16[128,1152]{1,0:T(8,128)(2,1)S(1)}, bf16[128,1152]{1,0:T(8,128)(2,1)S(1)}, u32[]{:S(2)}, u32[]{:S(2)}) %collective-permute-start.1) | collective-permute-done | bytes 294944 | tf_op jit(solution)/shard_map/ppermute | solution.py:14
  33.9 0.4 fusion.2
  34.3 0.2 reshape.11
  34.6 1.8 %gather_fusion = bf16[128,2,1152]{2,1,0:T(2,128)(2,1)S(1)} fusion(bf16[128,2,1152]{2,1,0:T(2,128)(2,1)S(1)} %reshape.11, s32[1024]{0:T(1024)S(1)} %pad_clamp_fusion), kind=kCustom, calls=%fused_computation | custom fusion | bytes 1180160 | tf_op jit(solution)/shard_map/jit(_take)/gather | solution.py:49
  36.4 0.6 broadcast_select_fusion
  37.0 0.0 copy-start.1
  37.0 42.2 %all_to_all.5 = bf16[128,2,1152]{2,1,0:T(2,128)(2,1)S(1)} all-to-all(bf16[128,2,1152]{2,1,0:T(2,128)(2,1)S(1)} %broadcast_select_fusion), channel_id=1, replica_groups=mesh['mid'=128,'sub'=4] {'mid'}, dimensions={0} | all-to-all | bytes 1179648 | tf_op jit(solution)/shard_map/all_to_all | solution.py:50
  79.2 0.2 reshape.12
  79.5 0.0 copy-done.1
  79.5 0.0 copy-start.4
  79.5 0.3 fusion.3
  79.8 0.1 broadcast_select_fusion.2
  79.9 1.9 %collective-permute-start.2 = (bf16[128,1152]{1,0:T(8,128)(2,1)S(1)}, bf16[128,1152]{1,0:T(8,128)(2,1)S(1)}, u32[]{:S(2)}, u32[]{:S(2)}) collective-permute-start(bf16[128,1152]{1,0:T(8,128)(2,1)S(1)} %get-tuple-element.7), channel_id=1, source_target_pairs={{0,2},{2,0},{1,3},{3,1},{4,6},{6,4},{5,7},{7,5},{8,10},{10,8},{9,1... | collective-permute-start | bytes 884744 | tf_op jit(solution)/shard_map/ppermute | solution.py:14
  81.8 15.5 %collective-permute-done.2 = bf16[128,1152]{1,0:T(8,128)(2,1)S(1)} collective-permute-done((bf16[128,1152]{1,0:T(8,128)(2,1)S(1)}, bf16[128,1152]{1,0:T(8,128)(2,1)S(1)}, u32[]{:S(2)}, u32[]{:S(2)}) %collective-permute-start.2) | collective-permute-done | bytes 294944 | tf_op jit(solution)/shard_map/ppermute | solution.py:14
  97.4 0.0 copy-done.4
  97.4 0.4 fusion.4
  97.7 0.8 broadcast_select_fusion.6
  98.5 1.9 %collective-permute-start.3 = (bf16[128,1152]{1,0:T(8,128)(2,1)S(1)}, bf16[128,1152]{1,0:T(8,128)(2,1)S(1)}, u32[]{:S(2)}, u32[]{:S(2)}) collective-permute-start(bf16[128,1152]{1,0:T(8,128)(2,1)S(1)} %get-tuple-element.5), channel_id=1, source_target_pairs={{0,1},{1,0},{2,3},{3,2},{4,5},{5,4},{6,7},{7,6},{8,9},{9,8},{10,11... | collective-permute-start | bytes 884744 | tf_op jit(solution)/shard_map/ppermute | solution.py:14
  100.4 7.5 %collective-permute-done.3 = bf16[128,1152]{1,0:T(8,128)(2,1)S(1)} collective-permute-done((bf16[128,1152]{1,0:T(8,128)(2,1)S(1)}, bf16[128,1152]{1,0:T(8,128)(2,1)S(1)}, u32[]{:S(2)}, u32[]{:S(2)}) %collective-permute-start.3) | collective-permute-done | bytes 294944 | tf_op jit(solution)/shard_map/ppermute | solution.py:14
  107.9 0.0 copy-start.2
  107.9 0.7 copy-done.2
  108.6 2.3 %fusion = bf16[768,1152]{0,1:T(8,128)(2,1)S(1)} fusion(bf16[768,256]{1,0:T(8,128)(2,1)} %param.12, bf16[128,1152]{1,0:T(8,128)(2,1)} %get-tuple-element.6, bf16[128,1152]{1,0:T(8,128)(2,1)} %copy-done.2, pred[]{:T(512)S(6)} %eq.4, bf16[1,2,256,256]{3,2,1,0:T(8,128)(2,1)} %param.11), kind=kOutput, calls=%fused_computation.2 | convolution fusion | flops 607813632 | bytes 2883585 | tf_op jit(solution)/shard_map/dot_general | solution.py:62
  110.9 2.2 %copy.8 = bf16[768,1152]{1,0:T(8,128)(2,1)} copy(bf16[768,1152]{0,1:T(8,128)(2,1)S(1)} %fusion) | data formatting | bytes 3538944 | tf_op jit(solution)/shard_map/convert_element_type | solution.py:62
  (3 shorter events, 0.0 us)
Async XLA Ops:
  0.0 1.5 %copy-start = (bf16[768,1152]{1,0:T(8,128)(2,1)S(1)}, bf16[768,1152]{1,0:T(8,128)(2,1)}, u32[]{:S(2)}) copy-start(bf16[768,1152]{1,0:T(8,128)(2,1)} %param.7) | copy-start | bytes 5308420
  3.2 4.9 %copy-start.5 = (s32[128]{0:T(128)S(1)}, s32[128]{0:T(128)}, u32[]{:S(2)}) copy-start(s32[128]{0:T(128)} %param.13) | copy-start | bytes 1540
  3.2 9.0 %copy-start.3 = (bf16[1,2,256,256]{3,2,1,0:T(8,128)(2,1)S(1)}, bf16[1,2,256,256]{3,2,1,0:T(8,128)(2,1)}, u32[]{:S(2)}) copy-start(bf16[1,2,256,256]{3,2,1,0:T(8,128)(2,1)} %param.9) | copy-start | bytes 786436
  3.3 8.9 %collective-permute-start = (bf16[128,1152]{1,0:T(8,128)(2,1)S(1)}, bf16[128,1152]{1,0:T(8,128)(2,1)S(1)}, u32[]{:S(2)}, u32[]{:S(2)}) collective-permute-start(bf16[128,1152]{1,0:T(8,128)(2,1)S(1)} %get-tuple-element.11), channel_id=1, source_target_pairs={{0,1},{1,0},{2,3},{3,2},{4,5},{5,4},{6,7},{7,6},{8,9},{9,8},{10,11... | collective-permute-start | bytes 884744 | tf_op jit(solution)/shard_map/ppermute | solution.py:14
  12.6 21.3 %collective-permute-start.1 = (bf16[128,1152]{1,0:T(8,128)(2,1)S(1)}, bf16[128,1152]{1,0:T(8,128)(2,1)S(1)}, u32[]{:S(2)}, u32[]{:S(2)}) collective-permute-start(bf16[128,1152]{1,0:T(8,128)(2,1)S(1)} %get-tuple-element.9), channel_id=1, source_target_pairs={{0,2},{2,0},{1,3},{3,1},{4,6},{6,4},{5,7},{7,5},{8,10},{10,8},{9,1... | collective-permute-start | bytes 884744 | tf_op jit(solution)/shard_map/ppermute | solution.py:14
  37.0 42.4 %copy-start.1 = (bf16[1,256,256]{2,1,0:T(8,128)(2,1)S(1)}, bf16[1,256,256]{2,1,0:T(8,128)(2,1)}, u32[]{:S(2)}) copy-start(bf16[1,256,256]{2,1,0:T(8,128)(2,1)} %param.10) | copy-start | bytes 393220
  79.5 17.9 %copy-start.4 = (bf16[1,2,256,256]{3,2,1,0:T(8,128)(2,1)S(1)}, bf16[1,2,256,256]{3,2,1,0:T(8,128)(2,1)}, u32[]{:S(2)}) copy-start(bf16[1,2,256,256]{3,2,1,0:T(8,128)(2,1)} %param.11) | copy-start | bytes 786436
  79.9 17.5 %collective-permute-start.2 = (bf16[128,1152]{1,0:T(8,128)(2,1)S(1)}, bf16[128,1152]{1,0:T(8,128)(2,1)S(1)}, u32[]{:S(2)}, u32[]{:S(2)}) collective-permute-start(bf16[128,1152]{1,0:T(8,128)(2,1)S(1)} %get-tuple-element.7), channel_id=1, source_target_pairs={{0,2},{2,0},{1,3},{3,1},{4,6},{6,4},{5,7},{7,5},{8,10},{10,8},{9,1... | collective-permute-start | bytes 884744 | tf_op jit(solution)/shard_map/ppermute | solution.py:14
  98.5 9.4 %collective-permute-start.3 = (bf16[128,1152]{1,0:T(8,128)(2,1)S(1)}, bf16[128,1152]{1,0:T(8,128)(2,1)S(1)}, u32[]{:S(2)}, u32[]{:S(2)}) collective-permute-start(bf16[128,1152]{1,0:T(8,128)(2,1)S(1)} %get-tuple-element.5), channel_id=1, source_target_pairs={{0,1},{1,0},{2,3},{3,2},{4,5},{5,4},{6,7},{7,6},{8,9},{9,8},{10,11... | collective-permute-start | bytes 884744 | tf_op jit(solution)/shard_map/ppermute | solution.py:14
  107.9 0.7 copy-start.2
where the time goes:
time: 114 us; the launch traced here: 113 us
  blocking collectives  42.2 us (37%)
  waiting for transfers between devices  39.9 us (35%)
  starting transfers between devices  17.1 us (15%)
  local copies, waits for them, and re-layouts  6.7 us (6%)
  matrix products  5.46 us (5%)
  other arithmetic  1.59 us (1%)
    all_to_all x1, blocking collectives, chain(): lax.all_to_all(ordered, 'mid', split_axis=0, concat_axis=0, tiled=True)  42.2 us
    ppermute x4, waiting for transfers between devices, from_partner(): return lax.ppermute(block, axis, route)  39.9 us
    ppermute x4, starting transfers between devices, from_partner(): return lax.ppermute(block, axis, route)  17.1 us
    dot_general x1, matrix products, chain(): jnp.dot(row_basis, coeffs, preferred_element_type=jnp.float32)  2.31 us
  transfers between devices with their start and end apart: 4, of which 4 were waited for; matrix products, arithmetic and copies ran while one was open for 0% of the time, Pallas kernels for 0%

commit v1 on v0

v1 whole, which is shorter than its diff:
```python
import jax
import jax.numpy as jnp
from jax import lax
from jax.experimental import pallas as pl
from jax.experimental.pallas import tpu as pltpu
from jax.sharding import PartitionSpec as P

MESH = pl.DeviceIdType.MESH
CHAIN = 55 << 20
EXPAND = 8 << 20
WIDTHS = (128,) * 9
LAG = (0, 3, 7, 11, 15, 18, 22, 25)
N = len(WIDTHS)
START = [sum(WIDTHS[:c]) for c in range(N)]
ORDER = [(s, c) for _, _, s, c in sorted((c + LAG[s], -s, s, c) for s in range(8) for c in range(N))]
RB0, RB1, ZH, YY, XC, LB1, LB0, SLOTS = 0, 1, 2, 3, 10, 17, 18, 19


def iota(shape, dim):
    return lax.broadcasted_iota(jnp.int32, shape, dim)


def onehot(hit):
    return jnp.where(hit, 1.0, 0.0).astype(jnp.bfloat16)


def mm(a, b):
    return jnp.dot(a, b, preferred_element_type=jnp.float32).astype(jnp.bfloat16)


def chain(
    sig_h, cb_h, rc_h, mc_h, lc_h, order, out, cb, rc, mc, lc, cbt, w0, w1, w2, w3, w4, p2,
    load, send, recv, *bufs,
):
    mid, sub = lax.axis_index("mid"), lax.axis_index("sub")
    core, zhi, y, x = mid % 2, (mid // 2) % 2, (mid // 4) % 8, mid // 32
    v0, v1 = sub % 2, sub // 2

    def cols(c):
        return slice(START[c], START[c] + WIDTHS[c])

    sig, own, outgo, come, near, ygot, xsend, xgot = (bufs[k * N : k * N + N] for k in range(8))

    def at(x_, y_, z_, c_):
        return ((x_ % 4 * 8 + y_ % 8) * 2 + z_ % 2) * 2 + c_ % 2, sub

    pair0 = (mid, sub + 1 - 2 * v0)
    pair1 = (mid, sub + 2 - 4 * v1)
    pairz = at(x, y, zhi + 1, core)
    ypeer = [at(x, y + k, zhi, core) for k in range(8)]
    xpeer = [at(x + j // 2, y, zhi, core + j % 2) for j in range(8)]
    ysrc = [at(x, y + 8 - k, zhi, core) for k in range(8)]
    xsrc = [at(x + 4 - j // 2, y, zhi, core + j % 2) for j in range(8)]

    barrier = pltpu.get_barrier_semaphore()
    greet = [pair0, pair1, pairz] + ysrc[1:] + xsrc[1:]
    for peer in greet:
        pl.semaphore_signal(barrier, inc=1, device_id=peer, device_id_type=MESH)

    loads = [pltpu.make_async_copy(cb_h, cb, load.at[0])]
    loads += [
        pltpu.make_async_copy(sig_h.at[:, cols(c)], sig[c], load.at[1 + c])
        for c in range(N)
    ]
    loads += [
        pltpu.make_async_copy(rc_h.at[0], rc, load.at[N + 1]),
        pltpu.make_async_copy(mc_h.at[0], mc, load.at[N + 2]),
        pltpu.make_async_copy(lc_h.at[0], lc, load.at[N + 3]),
    ]
    for copy in loads:
        copy.start()

    def half(v):
        return pl.ds(pl.multiple_of(v * 128, 128), 128)

    def swap(dst, src, rows, cols):
        for a, r in enumerate((rows, 1 - rows)):
            for b, q in enumerate((cols, 1 - cols)):
                dst[a * 128 : a * 128 + 128, b * 128 : b * 128 + 128] = src[half(r), half(q)]


    def copies(c):
        one = outgo[c]
        got = come[c]
        yield RB0, one.at[0], got.at[0], pair0
        yield RB1, one.at[1], got.at[1], pair1
        yield ZH, one.at[2], near[c].at[1], pairz
        for k in range(1, 8):
            yield YY + k - 1, near[c].at[:, pl.ds(k * 16, 16)], ygot[c].at[k], ypeer[k]
        for j in range(1, 8):
            yield XC + j - 1, xsend[c].at[j], xgot[c].at[j], xpeer[j]
        yield LB1, one.at[3], got.at[3], pair1
        yield LB0, one.at[4], got.at[4], pair0

    table = [
        {
            slot: pltpu.make_async_remote_copy(
                src_ref=src, dst_ref=dst, send_sem=send.at[c, slot], recv_sem=recv.at[c, slot],
                device_id=peer, device_id_type=MESH,
            )
            for slot, src, dst, peer in copies(c)
        }
        for c in range(N)
    ]

    def both(c, k):
        return jnp.concatenate([own[c][k], come[c][k]], axis=0)

    def split(c, k, value):
        outgo[c][k] = value[128:]
        own[c][k] = value[:128]

    def stage(s, c):
        hop = table[c]
        if s == 0:
            loads[1 + c].wait()
            split(c, 0, mm(cbt[...], sig[c][...]))
            hop[RB0].start()
        elif s == 1:
            hop[RB0].wait_recv()
            split(c, 1, mm(w0[...], both(c, 0)))
            hop[RB1].start()
        elif s == 2:
            hop[RB1].wait_recv()
            value = mm(w1[...], both(c, 1))
            outgo[c][2] = value[128:]
            near[c][0] = value[:128]
            hop[ZH].start()
        elif s == 3:
            hop[ZH].wait_recv()
            for k in (4, 3, 5, 2, 6, 1, 7):
                hop[YY + k - 1].start()
        elif s == 4:
            for k in range(1, 8):
                hop[YY + k - 1].wait_recv()
            value = jnp.concatenate(
                [near[c][0, 0:16], near[c][1, 0:16]] + [ygot[c][k].reshape(32, WIDTHS[c]) for k in range(1, 8)],
                axis=0,
            )
            xsend[c][...] = mm(p2[...], value).reshape(8, 32, WIDTHS[c])
            for j in (4, 5, 2, 3, 6, 7, 1):
                hop[XC + j - 1].start()
        elif s == 5:
            for j in range(1, 8):
                hop[XC + j - 1].wait_recv()
            value = jnp.concatenate([xsend[c][0]] + [xgot[c][j] for j in range(1, 8)], axis=0)
            split(c, 3, mm(w2[...], value))
            hop[LB1].start()
        elif s == 6:
            hop[LB1].wait_recv()
            split(c, 4, mm(w3[...], both(c, 3)))
            hop[LB0].start()
        else:
            hop[LB0].wait_recv()
            out[:, cols(c)] = mm(w4[...], both(c, 4))

    loads[0].wait()
    cbt[0:128] = cb[:, half(v0)].T
    cbt[128:256] = cb[:, half(1 - v0)].T

    def prepare():
        r = iota((256, 128), 0)
        dest = (
            ((((r >> 2) & 3) + x & 3) * 8 + (((r >> 4) & 7) + y & 7)) * 4
            + ((r >> 7) + zhi & 1) * 2
            + (((r >> 1) & 1) + core & 1)
        )
        piece = jnp.sum(
            jnp.where(iota((256, 128), 1) == dest, order[...].astype(jnp.float32), 0.0),
            axis=1, keepdims=True,
        ).astype(jnp.int32)
        row, col = iota((256, 256), 0), iota((256, 256), 1)
        pick = onehot(col == piece * 2 + (row & 1))
        p2[...] = onehot(
            col == ((row >> 2) & 7) * 32 + ((row >> 1) & 1) * 16 + (row >> 5) * 2 + (row & 1)
        )
        sx, sc, sy, sz = col >> 6, (col >> 5) & 1, (col >> 2) & 7, (col >> 1) & 1
        source = (
            ((x + 4 - sx & 3) * 8 + (y + 8 - sy & 7)) * 4 + (zhi + sz & 1) * 2 + (core + sc & 1)
        ) * 2 + (col & 1)
        place = onehot(row == source)
        for copy in loads[N + 1 :]:
            copy.wait()
        swap(w0, rc.at[0], v1, v0)
        for b, q in enumerate((v1, 1 - v1)):
            w3[:, b * 128 : b * 128 + 128] = rc[1, :, half(q)]
        w1[...] = mm(pick, w3[...])
        w4[...] = mm(mc[...], place)
        w2[0:128] = w4[half(v1), :]
        w2[128:256] = w4[half(1 - v1), :]
        swap(w3, lc.at[0], v0, v1)
        for b, q in enumerate((v0, 1 - v0)):
            w4[:, b * 128 : b * 128 + 128] = lc[1, :, half(q)]

    first = True
    for s, c in ORDER:
        if s == 0 and c == 0:
            loads[1].wait()
            split(0, 0, mm(cbt[...], sig[0][...]))
            pl.semaphore_wait(barrier, len(greet))
            table[0][RB0].start()
            continue
        if s == 1 and first:
            prepare()
            first = False
        stage(s, c)
    for hop in table:
        for copy in hop.values():
            copy.wait_send()


def expand(rb, c5, out, tile, sem):
    rows = tile.shape[1]
    copies = []
    for i in range(tile.shape[0]):
        block = slice(i * rows, i * rows + rows)
        tile[i] = mm(rb[block], c5[...])
        copies.append(pltpu.make_async_copy(tile.at[i], out.at[block], sem.at[i]))
        copies[-1].start()
    for copy in copies:
        copy.wait()


def local(signal, col_basis, right_coupling, middle_coupling, left_coupling, row_basis, node_order):
    bf = jnp.bfloat16
    V = pltpu.VMEM
    hbm = pl.BlockSpec(memory_space=pl.ANY)
    vmem = pl.BlockSpec(memory_space=V)
    coeffs = pl.pallas_call(
        chain,
        name="chain",
        out_shape=V((256, signal.shape[1]), bf),
        in_specs=[hbm] * 5 + [vmem],
        out_specs=vmem,
        scratch_shapes=[
            V((768, 256), bf), V((2, 256, 256), bf), V((256, 256), bf), V((2, 256, 256), bf), V((256, 768), bf),
        ]
        + [V((256, 256), bf)] * 6
        + [
            pltpu.SemaphoreType.DMA((N + 4,)),
            pltpu.SemaphoreType.DMA((N, SLOTS)),
            pltpu.SemaphoreType.DMA((N, SLOTS)),
        ]
        + [
            V((*shape, width), bf)
            for shape in (
                (768,), (5, 128), (5, 128), (5, 128), (2, 128), (8, 2, 16), (8, 32), (8, 32)
            )
            for width in WIDTHS
        ],
        compiler_params=pltpu.CompilerParams(collective_id=0, has_side_effects=True, vmem_limit_bytes=CHAIN),
    )(signal, col_basis, right_coupling, middle_coupling, left_coupling, node_order.reshape(1, 128))
    rows, block = row_basis.shape[0], 128
    return pl.pallas_call(
        expand,
        name="expand",
        out_shape=jax.ShapeDtypeStruct((rows, signal.shape[1]), bf),
        in_specs=[vmem, vmem],
        out_specs=hbm,
        scratch_shapes=[
            V((rows // block, block, signal.shape[1]), bf), pltpu.SemaphoreType.DMA((rows // block,))
        ],
        compiler_params=pltpu.CompilerParams(vmem_limit_bytes=EXPAND),
    )(row_basis, coeffs)


def solution(mesh):
    return jax.shard_map(
        local,
        mesh=mesh,
        in_specs=(
            P(("mid", "sub"), None),
            P(("mid", "sub"), None),
            P(("mid", "sub"), None, None, None),
            P(("mid", "sub"), None, None),
            P(("mid", "sub"), None, None, None),
            P(("mid", "sub"), None),
            P(),
        ),
        out_specs=P(("mid", "sub"), None),
        check_vma=False,
    )
```

time: 114 us -> 73.2 us (0.64)
  Pallas kernels: 0 us -> 73.1 us
  blocking collectives: 42.2 us -> 0 us
  waiting for transfers between devices: 39.9 us -> 0 us
  starting transfers between devices: 17.1 us -> 0 us
  local copies, waits for them, and re-layouts: 6.7 us -> 0.01 us
  matrix products: 5.46 us -> 0 us
  other arithmetic: 1.59 us -> 0 us
    pallas_call x0 -> x2, Pallas kernels: none -> 73.1 us  [the longest x1 71.5 us: local(): pl.pallas_call(chain, name='chain', out_shape=V((256, signal.shape[1]), b...]
    all_to_all x1 -> x0, blocking collectives: 42.2 us -> none  [chain(): lax.all_to_all(ordered, 'mid', split_axis=0, concat_axis=0, tiled=True)]
    ppermute x4 -> x0, waiting for transfers between devices: 39.9 us -> none  [from_partner(): return lax.ppermute(block, axis, route)]
    ppermute x4 -> x0, starting transfers between devices: 17.1 us -> none  [from_partner(): return lax.ppermute(block, axis, route)]
    dot_general x6 -> x0, matrix products: 5.46 us -> none  [the longest x1 2.31 us: chain(): jnp.dot(row_basis, coeffs, preferred_element_type=jnp.float32)]
    unnamed x12 -> x2, local copies, waits for them, and re-layouts: 2.22 us -> 0.01 us
    convert_element_type x1 -> x0, local copies, waits for them, and re-layouts: 2.21 us -> none  [chain(): jnp.dot(row_basis, coeffs, preferred_element_type=jnp.float32)]
    gather x1 -> x0, local copies, waits for them, and re-layouts: 1.83 us -> none  [chain(): ordered = jnp.take(pieces, node_order, axis=0)]
  transfers between devices with their start and end apart: 4 -> 0, of which waited for: 4 -> 0; matrix products, arithmetic and copies ran while one was open for 0% -> 0% of each run, Pallas kernels for 0% -> 0%
where the time goes in v1:
time: 73.2 us; the launch traced here: 73.1 us
  Pallas kernels  73.1 us (100%)
    pallas_call x1, Pallas kernels, local(): pl.pallas_call(chain, name='chain', out_shape=V((256, signal.shape[1]), b...  71.5 us
    pallas_call x1, Pallas kernels, local(): pl.pallas_call(expand, name='expand', out_shape=jax.ShapeDtypeStruct((row...  1.53 us

profile of v1, /device:TPU:1, one launch (start us, length us, event | category | flops | bytes accessed | tf_op | source)
XLA Modules:
  0.0 73.1 jit_solution(17793866609616612597)
XLA Ops:
  0.0 0.0 copy-start
  0.0 71.5 %chain.1.c5 = bf16[256,1152]{1,0:T(8,128)(2,1)S(1)} custom-call(bf16[768,1152]{1,0:T(8,128)(2,1)} %sig_h.1, bf16[768,256]{1,0:T(8,128)(2,1)} %cb_h.1, bf16[1,2,256,256]{3,2,1,0:T(8,128)(2,1)} %rc_h.1, bf16[1,256,256]{2,1,0:T(8,128)(2,1)} %mc_h.1, bf16[1,2,256,256]{3,2,1,0:T(8,128)(2,1)} %lc_h.1, s32[1,128]{1,0:T(1,128)} %bitcast.1), custom_call_target="tpu_custom_call" | custom-call | tf_op jit(solution)/shard_map/chain/pallas_call | solution.py:229
  71.6 0.0 copy-done
  71.6 1.5 %expand.1 = bf16[768,1152]{1,0:T(8,128)(2,1)} custom-call(bf16[768,256]{1,0:T(8,128)(2,1)S(1)} %copy-done, bf16[256,1152]{1,0:T(8,128)(2,1)S(1)} %chain.1.c5), custom_call_target="tpu_custom_call" | custom-call | tf_op jit(solution)/shard_map/expand/pallas_call | solution.py:254
Async XLA Ops:
  0.0 71.6 %copy-start = (bf16[768,256]{1,0:T(8,128)(2,1)S(1)}, bf16[768,256]{1,0:T(8,128)(2,1)}, u32[]{:S(2)}) copy-start(bf16[768,256]{1,0:T(8,128)(2,1)} %rb.1) | copy-start | bytes 1179652

commit v2 on v1

--- a/solution.py
+++ b/solution.py
@@ -9,11 +9,11 @@
 CHAIN = 55 << 20
 EXPAND = 8 << 20
 WIDTHS = (128,) * 9
-LAG = (0, 3, 7, 11, 15, 18, 22, 25)
+LAG = (0, 4, 8, 12, 16, 20, 24, 28)
 N = len(WIDTHS)
 START = [sum(WIDTHS[:c]) for c in range(N)]
 ORDER = [(s, c) for _, _, s, c in sorted((c + LAG[s], -s, s, c) for s in range(8) for c in range(N))]
-RB0, RB1, ZH, YY, XC, LB1, LB0, SLOTS = 0, 1, 2, 3, 10, 17, 18, 19
+RB0, RB1, ZH, YY, XC, LB1, LB0, SLOTS = 0, 1, 2, 3, 4, 5, 6, 7
 
 
 def iota(shape, dim):
@@ -30,7 +30,7 @@
 
 def chain(
     sig_h, cb_h, rc_h, mc_h, lc_h, order, out, cb, rc, mc, lc, cbt, w0, w1, w2, w3, w4, p2,
-    load, send, recv, *bufs,
+    sent, load, send, recv, *bufs,
 ):
     mid, sub = lax.axis_index("mid"), lax.axis_index("sub")
     core, zhi, y, x = mid % 2, (mid // 2) % 2, (mid // 4) % 8, mid // 32
@@ -79,29 +79,14 @@
                 dst[a * 128 : a * 128 + 128, b * 128 : b * 128 + 128] = src[half(r), half(q)]
 
 
-    def copies(c):
-        one = outgo[c]
-        got = come[c]
-        yield RB0, one.at[0], got.at[0], pair0
-        yield RB1, one.at[1], got.at[1], pair1
-        yield ZH, one.at[2], near[c].at[1], pairz
-        for k in range(1, 8):
-            yield YY + k - 1, near[c].at[:, pl.ds(k * 16, 16)], ygot[c].at[k], ypeer[k]
-        for j in range(1, 8):
-            yield XC + j - 1, xsend[c].at[j], xgot[c].at[j], xpeer[j]
-        yield LB1, one.at[3], got.at[3], pair1
-        yield LB0, one.at[4], got.at[4], pair0
-
-    table = [
-        {
-            slot: pltpu.make_async_remote_copy(
-                src_ref=src, dst_ref=dst, send_sem=send.at[c, slot], recv_sem=recv.at[c, slot],
-                device_id=peer, device_id_type=MESH,
-            )
-            for slot, src, dst, peer in copies(c)
-        }
-        for c in range(N)
-    ]
+    def remote(c, slot, src, dst, peer):
+        pltpu.make_async_remote_copy(
+            src_ref=src, dst_ref=dst, send_sem=send.at[0], recv_sem=recv.at[c, slot],
+            device_id=peer, device_id_type=MESH,
+        ).start()
+
+    def arrived(c, slot, dst):
+        pltpu.make_async_copy(dst, dst, recv.at[c, slot]).wait()
 
     def both(c, k):
         return jnp.concatenate([own[c][k], come[c][k]], axis=0)
@@ -111,47 +96,44 @@
         own[c][k] = value[:128]
 
     def stage(s, c):
-        hop = table[c]
         if s == 0:
             loads[1 + c].wait()
             split(c, 0, mm(cbt[...], sig[c][...]))
-            hop[RB0].start()
+            remote(c, RB0, outgo[c].at[0], come[c].at[0], pair0)
         elif s == 1:
-            hop[RB0].wait_recv()
+            arrived(c, RB0, come[c].at[0])
             split(c, 1, mm(w0[...], both(c, 0)))
-            hop[RB1].start()
+            remote(c, RB1, outgo[c].at[1], come[c].at[1], pair1)
         elif s == 2:
-            hop[RB1].wait_recv()
+            arrived(c, RB1, come[c].at[1])
             value = mm(w1[...], both(c, 1))
             outgo[c][2] = value[128:]
             near[c][0] = value[:128]
-            hop[ZH].start()
+            remote(c, ZH, outgo[c].at[2], near[c].at[1], pairz)
         elif s == 3:
-            hop[ZH].wait_recv()
+            arrived(c, ZH, near[c].at[1])
             for k in (4, 3, 5, 2, 6, 1, 7):
-                hop[YY + k - 1].start()
+                remote(c, YY, near[c].at[:, pl.ds(k * 16, 16)], ygot[c].at[k], ypeer[k])
         elif s == 4:
-            for k in range(1, 8):
-                hop[YY + k - 1].wait_recv()
+            arrived(c, YY, ygot[c].at[1:8])
             value = jnp.concatenate(
                 [near[c][0, 0:16], near[c][1, 0:16]] + [ygot[c][k].reshape(32, WIDTHS[c]) for k in range(1, 8)],
                 axis=0,
             )
             xsend[c][...] = mm(p2[...], value).reshape(8, 32, WIDTHS[c])
             for j in (4, 5, 2, 3, 6, 7, 1):
-                hop[XC + j - 1].start()
+                remote(c, XC, xsend[c].at[j], xgot[c].at[j], xpeer[j])
         elif s == 5:
-            for j in range(1, 8):
-                hop[XC + j - 1].wait_recv()
+            arrived(c, XC, xgot[c].at[1:8])
             value = jnp.concatenate([xsend[c][0]] + [xgot[c][j] for j in range(1, 8)], axis=0)
             split(c, 3, mm(w2[...], value))
-            hop[LB1].start()
+            remote(c, LB1, outgo[c].at[3], come[c].at[3], pair1)
         elif s == 6:
-            hop[LB1].wait_recv()
+            arrived(c, LB1, come[c].at[3])
             split(c, 4, mm(w3[...], both(c, 3)))
-            hop[LB0].start()
+            remote(c, LB0, outgo[c].at[4], come[c].at[4], pair0)
         else:
-            hop[LB0].wait_recv()
+            arrived(c, LB0, come[c].at[4])
             out[:, cols(c)] = mm(w4[...], both(c, 4))
 
     loads[0].wait()
@@ -198,15 +180,13 @@
             loads[1].wait()
             split(0, 0, mm(cbt[...], sig[0][...]))
             pl.semaphore_wait(barrier, len(greet))
-            table[0][RB0].start()
+            remote(0, RB0, outgo[0].at[0], come[0].at[0], pair0)
             continue
         if s == 1 and first:
             prepare()
             first = False
         stage(s, c)
-    for hop in table:
-        for copy in hop.values():
-            copy.wait_send()
+    pltpu.make_async_copy(sent, sent, send.at[0]).wait()
 
 
 def expand(rb, c5, out, tile, sem):
@@ -237,8 +217,9 @@
         ]
         + [V((256, 256), bf)] * 6
         + [
+            V((1088, signal.shape[1]), bf),
             pltpu.SemaphoreType.DMA((N + 4,)),
-            pltpu.SemaphoreType.DMA((N, SLOTS)),
+            pltpu.SemaphoreType.DMA((1,)),
             pltpu.SemaphoreType.DMA((N, SLOTS)),
         ]
         + [

time: 73.2 us -> 70.4 us (0.962)
  the two profiles are of different devices: /device:TPU:1 before, /device:TPU:8 now
where the time goes in v2:
time: 70.4 us; the launch traced here: 70.3 us
  Pallas kernels  70.3 us (100%)
    pallas_call x1, Pallas kernels, local(): pl.pallas_call(chain, name='chain', out_shape=V((256, signal.shape[1]), b...  68.7 us
    pallas_call x1, Pallas kernels, local(): pl.pallas_call(expand, name='expand', out_shape=jax.ShapeDtypeStruct((row...  1.53 us

profile of v2, /device:TPU:8, one launch (start us, length us, event | category | flops | bytes accessed | tf_op | source)
XLA Modules:
  0.0 70.3 jit_solution(8138085355657780973)
XLA Ops:
  0.0 0.0 copy-start
  0.0 68.7 %chain.1.c5 = bf16[256,1152]{1,0:T(8,128)(2,1)S(1)} custom-call(bf16[768,1152]{1,0:T(8,128)(2,1)} %sig_h.1, bf16[768,256]{1,0:T(8,128)(2,1)} %cb_h.1, bf16[1,2,256,256]{3,2,1,0:T(8,128)(2,1)} %rc_h.1, bf16[1,256,256]{2,1,0:T(8,128)(2,1)} %mc_h.1, bf16[1,2,256,256]{3,2,1,0:T(8,128)(2,1)} %lc_h.1, s32[1,128]{1,0:T(1,128)} %bitcast.1), custom_call_target="tpu_custom_call" | custom-call | tf_op jit(solution)/shard_map/chain/pallas_call | solution.py:209
  68.7 0.0 copy-done
  68.7 1.5 %expand.1 = bf16[768,1152]{1,0:T(8,128)(2,1)} custom-call(bf16[768,256]{1,0:T(8,128)(2,1)S(1)} %copy-done, bf16[256,1152]{1,0:T(8,128)(2,1)S(1)} %chain.1.c5), custom_call_target="tpu_custom_call" | custom-call | tf_op jit(solution)/shard_map/expand/pallas_call | solution.py:235
Async XLA Ops:
  0.0 68.7 %copy-start = (bf16[768,256]{1,0:T(8,128)(2,1)S(1)}, bf16[768,256]{1,0:T(8,128)(2,1)}, u32[]{:S(2)}) copy-start(bf16[768,256]{1,0:T(8,128)(2,1)} %rb.1) | copy-start | bytes 1179652

commit v3 on v2

--- a/solution.py
+++ b/solution.py
@@ -9,7 +9,7 @@
 CHAIN = 55 << 20
 EXPAND = 8 << 20
 WIDTHS = (128,) * 9
-LAG = (0, 4, 8, 12, 16, 20, 24, 28)
+LAG = (0, 2, 5, 8, 12, 14, 17, 21)
 N = len(WIDTHS)
 START = [sum(WIDTHS[:c]) for c in range(N)]
 ORDER = [(s, c) for _, _, s, c in sorted((c + LAG[s], -s, s, c) for s in range(8) for c in range(N))]
@@ -29,7 +29,7 @@
 
 
 def chain(
-    sig_h, cb_h, rc_h, mc_h, lc_h, order, out, cb, rc, mc, lc, cbt, w0, w1, w2, w3, w4, p2,
+    sig_h, cb_h, rc_h, mc_h, lc_h, order_h, out, order, sig, cb, mats, cbt, w0, w1, w2, w3, w4, p2,
     sent, load, send, recv, *bufs,
 ):
     mid, sub = lax.axis_index("mid"), lax.axis_index("sub")
@@ -39,7 +39,21 @@
     def cols(c):
         return slice(START[c], START[c] + WIDTHS[c])
 
-    sig, own, outgo, come, near, ygot, xsend, xgot = (bufs[k * N : k * N + N] for k in range(8))
+    own, outgo, come, near, ygot, xsend, xgot = (bufs[k * N : k * N + N] for k in range(7))
+    rc, mc, lc = mats.at[0:2], mats.at[2], mats.at[3:5]
+
+    loads = [pltpu.make_async_copy(cb_h, cb, load.at[0])]
+    loads += [
+        pltpu.make_async_copy(sig_h.at[:, cols(c)], sig.at[c], load.at[min(c, 1) + 1]) for c in range(N)
+    ]
+    loads += [
+        pltpu.make_async_copy(rc_h.at[0], rc, load.at[3]),
+        pltpu.make_async_copy(mc_h.at[0], mc, load.at[3]),
+        pltpu.make_async_copy(lc_h.at[0], lc, load.at[3]),
+        pltpu.make_async_copy(order_h, order, load.at[4]),
+    ]
+    for copy in loads[:2]:
+        copy.start()
 
     def at(x_, y_, z_, c_):
         return ((x_ % 4 * 8 + y_ % 8) * 2 + z_ % 2) * 2 + c_ % 2, sub
@@ -57,19 +71,6 @@
     for peer in greet:
         pl.semaphore_signal(barrier, inc=1, device_id=peer, device_id_type=MESH)
 
-    loads = [pltpu.make_async_copy(cb_h, cb, load.at[0])]
-    loads += [
-        pltpu.make_async_copy(sig_h.at[:, cols(c)], sig[c], load.at[1 + c])
-        for c in range(N)
-    ]
-    loads += [
-        pltpu.make_async_copy(rc_h.at[0], rc, load.at[N + 1]),
-        pltpu.make_async_copy(mc_h.at[0], mc, load.at[N + 2]),
-        pltpu.make_async_copy(lc_h.at[0], lc, load.at[N + 3]),
-    ]
-    for copy in loads:
-        copy.start()
-
     def half(v):
         return pl.ds(pl.multiple_of(v * 128, 128), 128)
 
@@ -97,8 +98,9 @@
 
     def stage(s, c):
         if s == 0:
-            loads[1 + c].wait()
-            split(c, 0, mm(cbt[...], sig[c][...]))
+            if c == 1:
+                pltpu.make_async_copy(sig.at[1:N], sig.at[1:N], load.at[2]).wait()
+            split(c, 0, mm(cbt[...], sig[c]))
             remote(c, RB0, outgo[c].at[0], come[c].at[0], pair0)
         elif s == 1:
             arrived(c, RB0, come[c].at[0])
@@ -137,10 +139,13 @@
             out[:, cols(c)] = mm(w4[...], both(c, 4))
 
     loads[0].wait()
+    for copy in loads[2:]:
+        copy.start()
     cbt[0:128] = cb[:, half(v0)].T
     cbt[128:256] = cb[:, half(1 - v0)].T
 
     def prepare():
+        loads[-1].wait()
         r = iota((256, 128), 0)
         dest = (
             ((((r >> 2) & 3) + x & 3) * 8 + (((r >> 4) & 7) + y & 7)) * 4
@@ -161,8 +166,7 @@
             ((x + 4 - sx & 3) * 8 + (y + 8 - sy & 7)) * 4 + (zhi + sz & 1) * 2 + (core + sc & 1)
         ) * 2 + (col & 1)
         place = onehot(row == source)
-        for copy in loads[N + 1 :]:
-            copy.wait()
+        pltpu.make_async_copy(mats, mats, load.at[3]).wait()
         swap(w0, rc.at[0], v1, v0)
         for b, q in enumerate((v1, 1 - v1)):
             w3[:, b * 128 : b * 128 + 128] = rc[1, :, half(q)]
@@ -178,7 +182,7 @@
     for s, c in ORDER:
         if s == 0 and c == 0:
             loads[1].wait()
-            split(0, 0, mm(cbt[...], sig[0][...]))
+            split(0, 0, mm(cbt[...], sig[0]))
             pl.semaphore_wait(barrier, len(greet))
             remote(0, RB0, outgo[0].at[0], come[0].at[0], pair0)
             continue
@@ -210,22 +214,22 @@
         chain,
         name="chain",
         out_shape=V((256, signal.shape[1]), bf),
-        in_specs=[hbm] * 5 + [vmem],
+        in_specs=[hbm] * 6,
         out_specs=vmem,
         scratch_shapes=[
-            V((768, 256), bf), V((2, 256, 256), bf), V((256, 256), bf), V((2, 256, 256), bf), V((256, 768), bf),
+            V((1, 128), jnp.int32), V((N, 768, WIDTHS[0]), bf), V((768, 256), bf), V((5, 256, 256), bf), V((256, 768), bf),
         ]
         + [V((256, 256), bf)] * 6
         + [
             V((1088, signal.shape[1]), bf),
-            pltpu.SemaphoreType.DMA((N + 4,)),
+            pltpu.SemaphoreType.DMA((5,)),
             pltpu.SemaphoreType.DMA((1,)),
             pltpu.SemaphoreType.DMA((N, SLOTS)),
         ]
         + [
             V((*shape, width), bf)
             for shape in (
-                (768,), (5, 128), (5, 128), (5, 128), (2, 128), (8, 2, 16), (8, 32), (8, 32)
+                (5, 128), (5, 128), (5, 128), (2, 128), (8, 2, 16), (8, 32), (8, 32)
             )
             for width in WIDTHS
         ],

time: 70.4 us -> 67.6 us (0.960)
  the two profiles are of different devices: /device:TPU:8 before, /device:TPU:1 now
where the time goes in v3:
time: 67.6 us; the launch traced here: 67.4 us
  Pallas kernels  67.4 us (100%)
    pallas_call x1, Pallas kernels, local(): pl.pallas_call(chain, name='chain', out_shape=V((256, signal.shape[1]), b...  65.8 us
    pallas_call x1, Pallas kernels, local(): pl.pallas_call(expand, name='expand', out_shape=jax.ShapeDtypeStruct((row...  1.53 us

profile of v3, /device:TPU:1, one launch (start us, length us, event | category | flops | bytes accessed | tf_op | source)
XLA Modules:
  0.0 67.4 jit_solution(14872206840950931074)
XLA Ops:
  0.0 0.0 copy-start
  0.0 65.8 %chain.1.c5 = bf16[256,1152]{1,0:T(8,128)(2,1)S(1)} custom-call(bf16[768,1152]{1,0:T(8,128)(2,1)} %sig_h.1, bf16[768,256]{1,0:T(8,128)(2,1)} %cb_h.1, bf16[1,2,256,256]{3,2,1,0:T(8,128)(2,1)} %rc_h.1, bf16[1,256,256]{2,1,0:T(8,128)(2,1)} %mc_h.1, bf16[1,2,256,256]{3,2,1,0:T(8,128)(2,1)} %lc_h.1, s32[1,128]{1,0:T(1,128)} %bitcast.1), custom_call_target="tpu_custom_call" | custom-call | tf_op jit(solution)/shard_map/chain/pallas_call | solution.py:213
  65.8 0.0 copy-done
  65.8 1.5 %expand.1 = bf16[768,1152]{1,0:T(8,128)(2,1)} custom-call(bf16[768,256]{1,0:T(8,128)(2,1)S(1)} %copy-done, bf16[256,1152]{1,0:T(8,128)(2,1)S(1)} %chain.1.c5), custom_call_target="tpu_custom_call" | custom-call | tf_op jit(solution)/shard_map/expand/pallas_call | solution.py:239
Async XLA Ops:
  0.0 65.8 %copy-start = (bf16[768,256]{1,0:T(8,128)(2,1)S(1)}, bf16[768,256]{1,0:T(8,128)(2,1)}, u32[]{:S(2)}) copy-start(bf16[768,256]{1,0:T(8,128)(2,1)} %rb.1) | copy-start | bytes 1179652

commit v4 on v3

--- a/solution.py
+++ b/solution.py
@@ -9,7 +9,7 @@
 CHAIN = 55 << 20
 EXPAND = 8 << 20
 WIDTHS = (128,) * 9
-LAG = (0, 2, 5, 8, 12, 14, 17, 21)
+LAG = (0, 2, 5, 8, 11, 14, 17, 21)
 N = len(WIDTHS)
 START = [sum(WIDTHS[:c]) for c in range(N)]
 ORDER = [(s, c) for _, _, s, c in sorted((c + LAG[s], -s, s, c) for s in range(8) for c in range(N))]
@@ -92,26 +92,25 @@
     def both(c, k):
         return jnp.concatenate([own[c][k], come[c][k]], axis=0)
 
-    def split(c, k, value):
-        outgo[c][k] = value[128:]
-        own[c][k] = value[:128]
+    def split(c, k, slot, peer, matrix, value):
+        outgo[c][k] = mm(matrix[128:256], value)
+        remote(c, slot, outgo[c].at[k], come[c].at[k], peer)
+        own[c][k] = mm(matrix[0:128], value)
 
     def stage(s, c):
         if s == 0:
             if c == 1:
                 pltpu.make_async_copy(sig.at[1:N], sig.at[1:N], load.at[2]).wait()
-            split(c, 0, mm(cbt[...], sig[c]))
-            remote(c, RB0, outgo[c].at[0], come[c].at[0], pair0)
+            split(c, 0, RB0, pair0, cbt, sig[c])
         elif s == 1:
             arrived(c, RB0, come[c].at[0])
-            split(c, 1, mm(w0[...], both(c, 0)))
-            remote(c, RB1, outgo[c].at[1], come[c].at[1], pair1)
+            split(c, 1, RB1, pair1, w0, both(c, 0))
         elif s == 2:
             arrived(c, RB1, come[c].at[1])
-            value = mm(w1[...], both(c, 1))
-            outgo[c][2] = value[128:]
-            near[c][0] = value[:128]
+            value = both(c, 1)
+            outgo[c][2] = mm(w1[128:256], value)
             remote(c, ZH, outgo[c].at[2], near[c].at[1], pairz)
+            near[c][0] = mm(w1[0:128], value)
         elif s == 3:
             arrived(c, ZH, near[c].at[1])
             for k in (4, 3, 5, 2, 6, 1, 7):
@@ -128,12 +127,10 @@
         elif s == 5:
             arrived(c, XC, xgot[c].at[1:8])
             value = jnp.concatenate([xsend[c][0]] + [xgot[c][j] for j in range(1, 8)], axis=0)
-            split(c, 3, mm(w2[...], value))
-            remote(c, LB1, outgo[c].at[3], come[c].at[3], pair1)
+            split(c, 3, LB1, pair1, w2, value)
         elif s == 6:
             arrived(c, LB1, come[c].at[3])
-            split(c, 4, mm(w3[...], both(c, 3)))
-            remote(c, LB0, outgo[c].at[4], come[c].at[4], pair0)
+            split(c, 4, LB0, pair0, w3, both(c, 3))
         else:
             arrived(c, LB0, come[c].at[4])
             out[:, cols(c)] = mm(w4[...], both(c, 4))
@@ -182,9 +179,8 @@
     for s, c in ORDER:
         if s == 0 and c == 0:
             loads[1].wait()
-            split(0, 0, mm(cbt[...], sig[0]))
             pl.semaphore_wait(barrier, len(greet))
-            remote(0, RB0, outgo[0].at[0], come[0].at[0], pair0)
+            split(0, 0, RB0, pair0, cbt, sig[0])
             continue
         if s == 1 and first:
             prepare()

time: 67.6 us -> 65.8 us (0.973)
  Pallas kernels: 67.4 us -> 65.6 us
    pallas_call x1, Pallas kernels: 65.8 us -> 64.1 us  [local(): pl.pallas_call(chain, name='chain', out_shape=V((256, signal.shape[1]), b...]
where the time goes in v4:
time: 65.8 us; the launch traced here: 65.6 us
  Pallas kernels  65.6 us (100%)
    pallas_call x1, Pallas kernels, local(): pl.pallas_call(chain, name='chain', out_shape=V((256, signal.shape[1]), b...  64.1 us
    pallas_call x1, Pallas kernels, local(): pl.pallas_call(expand, name='expand', out_shape=jax.ShapeDtypeStruct((row...  1.53 us

profile of v4, /device:TPU:1, one launch (start us, length us, event | category | flops | bytes accessed | tf_op | source)
XLA Modules:
  0.0 65.6 jit_solution(14496882321156299308)
XLA Ops:
  0.0 0.0 copy-start
  0.0 64.1 %chain.1.c5 = bf16[256,1152]{1,0:T(8,128)(2,1)S(1)} custom-call(bf16[768,1152]{1,0:T(8,128)(2,1)} %sig_h.1, bf16[768,256]{1,0:T(8,128)(2,1)} %cb_h.1, bf16[1,2,256,256]{3,2,1,0:T(8,128)(2,1)} %rc_h.1, bf16[1,256,256]{2,1,0:T(8,128)(2,1)} %mc_h.1, bf16[1,2,256,256]{3,2,1,0:T(8,128)(2,1)} %lc_h.1, s32[1,128]{1,0:T(1,128)} %bitcast.1), custom_call_target="tpu_custom_call" | custom-call | tf_op jit(solution)/shard_map/chain/pallas_call | solution.py:209
  64.1 0.0 copy-done
  64.1 1.5 %expand.1 = bf16[768,1152]{1,0:T(8,128)(2,1)} custom-call(bf16[768,256]{1,0:T(8,128)(2,1)S(1)} %copy-done, bf16[256,1152]{1,0:T(8,128)(2,1)S(1)} %chain.1.c5), custom_call_target="tpu_custom_call" | custom-call | tf_op jit(solution)/shard_map/expand/pallas_call | solution.py:235
Async XLA Ops:
  0.0 64.1 %copy-start = (bf16[768,256]{1,0:T(8,128)(2,1)S(1)}, bf16[768,256]{1,0:T(8,128)(2,1)}, u32[]{:S(2)}) copy-start(bf16[768,256]{1,0:T(8,128)(2,1)} %rb.1) | copy-start | bytes 1179652

commit v5 on v4

--- a/solution.py
+++ b/solution.py
@@ -231,7 +231,7 @@
         ],
         compiler_params=pltpu.CompilerParams(collective_id=0, has_side_effects=True, vmem_limit_bytes=CHAIN),
     )(signal, col_basis, right_coupling, middle_coupling, left_coupling, node_order.reshape(1, 128))
-    rows, block = row_basis.shape[0], 128
+    rows, block = row_basis.shape[0], 96
     return pl.pallas_call(
         expand,
         name="expand",

time: 65.8 us -> 65.9 us (level)
  no operation moved by 1% of the time
where the time goes in v5:
time: 65.9 us; the launch traced here: 65.8 us
  Pallas kernels  65.8 us (100%)
    pallas_call x1, Pallas kernels, local(): pl.pallas_call(chain, name='chain', out_shape=V((256, signal.shape[1]), b...  64.1 us
    pallas_call x1, Pallas kernels, local(): pl.pallas_call(expand, name='expand', out_shape=jax.ShapeDtypeStruct((row...  1.67 us

profile of v5, /device:TPU:1, one launch (start us, length us, event | category | flops | bytes accessed | tf_op | source)
XLA Modules:
  0.0 65.8 jit_solution(4932882120491702154)
XLA Ops:
  0.0 0.0 copy-start
  0.0 64.1 %chain.1.c5 = bf16[256,1152]{1,0:T(8,128)(2,1)S(1)} custom-call(bf16[768,1152]{1,0:T(8,128)(2,1)} %sig_h.1, bf16[768,256]{1,0:T(8,128)(2,1)} %cb_h.1, bf16[1,2,256,256]{3,2,1,0:T(8,128)(2,1)} %rc_h.1, bf16[1,256,256]{2,1,0:T(8,128)(2,1)} %mc_h.1, bf16[1,2,256,256]{3,2,1,0:T(8,128)(2,1)} %lc_h.1, s32[1,128]{1,0:T(1,128)} %bitcast.1), custom_call_target="tpu_custom_call" | custom-call | tf_op jit(solution)/shard_map/chain/pallas_call | solution.py:209
  64.1 0.0 copy-done
  64.1 1.7 %expand.1 = bf16[768,1152]{1,0:T(8,128)(2,1)} custom-call(bf16[768,256]{1,0:T(8,128)(2,1)S(1)} %copy-done, bf16[256,1152]{1,0:T(8,128)(2,1)S(1)} %chain.1.c5), custom_call_target="tpu_custom_call" | custom-call | tf_op jit(solution)/shard_map/expand/pallas_call | solution.py:235
Async XLA Ops:
  0.0 64.1 %copy-start = (bf16[768,256]{1,0:T(8,128)(2,1)S(1)}, bf16[768,256]{1,0:T(8,128)(2,1)}, u32[]{:S(2)}) copy-start(bf16[768,256]{1,0:T(8,128)(2,1)} %rb.1) | copy-start | bytes 1179652
